TPU v7x, 256 devices: a whole 4x4x8 slice. The times are simulated.
256 devices in a mesh: cam: 2 (over x_lo), band: 32 (over z, y), obj: 4 (over x_hi, core).
Axes of the slice: x: 4 (x_hi: 2, x_lo: 2; x = x_hi * 2 + x_lo), y: 4, z: 8, core: 2. Of those that a mesh axis runs over, the one named last changes fastest.
Arguments:
- queries: bfloat16 [4, 6, 32, 128, 1280], P('obj', 'cam', 'band'), may hold values from -6 to 6
- keys: bfloat16 [4, 6, 32, 128, 1280], P('obj', 'cam', 'band'), may hold values from -6 to 6
- values: bfloat16 [4, 6, 32, 128, 1280], P('obj', 'cam', 'band'), may hold values from -6 to 6
- d_out: bfloat16 [4, 6, 32, 128, 2432], P('obj', 'cam', 'band'), may hold values from -6 to 6
- w_out: bfloat16 [1280, 2432], P(('band', 'obj'), 'cam'), may hold values from -0.15625 to 0.15625
Outputs:
- grad_q: bfloat16 [4, 6, 32, 128, 1280], P('obj', 'cam', 'band')
- grad_k: bfloat16 [4, 6, 32, 128, 1280], P('obj', 'cam', 'band')
- grad_v: bfloat16 [4, 6, 32, 128, 1280], P('obj', 'cam', 'band')
- grad_wo: float32 [1280, 2432], P(('band', 'obj'), 'cam')
All inputs are finite; a program needn't handle non-finite values.
Results may differ from a plain program's by a relative error of at most 0.0095.
Values may be sent and summed in bfloat16 or wider, within the bound.
A program may use at most 128 MiB of HBM per device.

v0:
```python
import jax
import jax.numpy as jnp
from jax import lax
from jax.sharding import PartitionSpec as P


def to_pairs(x):
    objects, views, rows, cols, width = x.shape
    grouped = x.transpose(0, 2, 1, 3, 4).reshape(objects * rows, views * cols, width // 128, 128)
    return grouped.transpose(2, 0, 1, 3)


def from_pairs(x, objects, views, rows, cols):
    width = x.shape[0] * 128
    merged = x.transpose(1, 2, 0, 3).reshape(objects, rows, views, cols, width)
    return merged.transpose(0, 2, 1, 3, 4)


def pair_backward(parts):
    q_pair, k_pair, v_pair, d_pair = parts
    groups, n_query = (q_pair.shape[0], q_pair.shape[1])
    n_key = k_pair.shape[1]
    q_heads = q_pair.reshape(groups, n_query, 2, 64)
    k_heads = k_pair.reshape(groups, n_key, 2, 64)
    v_heads = v_pair.reshape(groups, n_key, 2, 64)
    d_heads = d_pair.reshape(groups, n_query, 2, 64)
    scores = (
        jnp.einsum("gqhe,gkhe->ghqk", q_heads, k_heads, preferred_element_type=jnp.float32) * 0.125
    )
    top = jnp.max(scores, axis=-1, keepdims=True)
    expd = jnp.exp(scores - top)
    probs = expd / jnp.sum(expd, axis=-1, keepdims=True)
    probs_b = probs.astype(jnp.bfloat16)
    att = jnp.einsum(
        "ghqk,gkhe->gqhe", probs_b, v_heads, preferred_element_type=jnp.float32
    ).astype(jnp.bfloat16)
    d_probs = jnp.einsum("gqhe,gkhe->ghqk", d_heads, v_heads, preferred_element_type=jnp.float32)
    delta = jnp.sum(probs * d_probs, axis=-1, keepdims=True)
    d_scores_b = (probs * (d_probs - delta)).astype(jnp.bfloat16)
    grad_q = (
        jnp.einsum("ghqk,gkhe->gqhe", d_scores_b, k_heads, preferred_element_type=jnp.float32)
        * 0.125
    )
    grad_k = (
        jnp.einsum("ghqk,gqhe->gkhe", d_scores_b, q_heads, preferred_element_type=jnp.float32)
        * 0.125
    )
    grad_v = jnp.einsum("ghqk,gqhe->gkhe", probs_b, d_heads, preferred_element_type=jnp.float32)
    return (
        grad_q.astype(jnp.bfloat16).reshape(groups, n_query, 128),
        grad_k.reshape(groups, n_key, 128),
        grad_v.reshape(groups, n_key, 128),
        att.reshape(groups, n_query, 128),
    )


def attend(q_part, k_part, v_part, d_part):
    objects, q_views, rows, cols, width = q_part.shape
    k_views = k_part.shape[1]
    results = lax.map(
        pair_backward, (to_pairs(q_part), to_pairs(k_part), to_pairs(v_part), to_pairs(d_part))
    )
    grad_q = from_pairs(results[0], objects, q_views, rows, cols)
    grad_k = from_pairs(results[1], objects, k_views, rows, cols)
    grad_v = from_pairs(results[2], objects, k_views, rows, cols)
    att = from_pairs(results[3], objects, q_views, rows, cols)
    return (grad_q, grad_k, grad_v, att)


def body(queries, keys, values, d_out, w_out):
    objects, views, rows, cols, width = queries.shape
    model_width = d_out.shape[4]
    flat_out = d_out.reshape(-1, model_width)
    total = flat_out.shape[0] * lax.axis_size("cam") * lax.axis_size("band") * lax.axis_size("obj")
    full_cols = lax.all_gather(w_out, "cam", axis=1, tiled=True)
    d_att = lax.dot_general(
        flat_out,
        lax.all_gather(full_cols, ("band", "obj"), axis=0, tiled=True),
        (((1,), (1,)), ((), ())),
        preferred_element_type=jnp.float32,
    )
    d_att = d_att.astype(jnp.bfloat16).reshape(objects, views, rows, cols, width)
    all_keys, all_values = (
        lax.all_gather(keys, "cam", axis=1, tiled=True),
        lax.all_gather(values, "cam", axis=1, tiled=True),
    )
    grad_q, partial_k, partial_v, att = attend(queries, all_keys, all_values, d_att)
    summed_k, summed_v = (
        lax.psum_scatter(partial_k, "cam", scatter_dimension=1, tiled=True),
        lax.psum_scatter(partial_v, "cam", scatter_dimension=1, tiled=True),
    )
    grad_k = summed_k.astype(jnp.bfloat16)
    grad_v = summed_v.astype(jnp.bfloat16)
    flat_att = att.reshape(-1, width)
    row_sums = lax.psum_scatter(
        lax.dot_general(
            flat_att, flat_out, (((0,), (0,)), ((), ())), preferred_element_type=jnp.float32
        ),
        ("band", "obj"),
        scatter_dimension=0,
        tiled=True,
    )
    grad_wo = lax.psum_scatter(
        row_sums.astype(jnp.bfloat16), "cam", scatter_dimension=1, tiled=True
    ).astype(jnp.float32)
    grad_wo = grad_wo * float(total) ** (-0.5)
    return (grad_q, grad_k, grad_v, grad_wo)


def solution(mesh):
    placed = (
        P("obj", "cam", "band", None, None),
        P("obj", "cam", "band", None, None),
        P("obj", "cam", "band", None, None),
        P("obj", "cam", "band", None, None),
        P(("band", "obj"), "cam"),
    )
    return jax.shard_map(
        body,
        mesh=mesh,
        in_specs=placed,
        out_specs=(
            P("obj", "cam", "band", None, None),
            P("obj", "cam", "band", None, None),
            P("obj", "cam", "band", None, None),
            P(("band", "obj"), "cam"),
        ),
        check_vma=False,
    )
```

profile of v0, /device:TPU:1, one launch (start us, length us, event | category | flops | bytes accessed | tf_op | source)
XLA Modules:
  0.0 1258.2 jit_solution(13432922650038172726)
XLA Ops:
  8.7 4.4 all-gather
  14.0 2.8 copy.30
  19.7 30.4 %all-gather.8.cloned.1.call-done = bf16[1,6,1,128,1280]{4,3,2,0,1:T(8,128)(2,1)} async-done(((bf16[1,3,1,128,1280]{4,3,2,0,1:T(8,128)(2,1)}), bf16[1,6,1,128,1280]{4,3,2,0,1:T(8,128)(2,1)}) %all-gather.8.cloned.1.call-update) | async-done | bytes 1966096 | tf_op jit(solution)/shard_map/all_gather | solution.py:85
  50.1 4.5 copy.34
  54.6 5.4 reshape_transpose.11
  60.0 29.6 %all-gather.6.cloned.1.call-done = bf16[1,6,1,128,1280]{4,3,2,0,1:T(8,128)(2,1)} async-done(((bf16[1,3,1,128,1280]{4,3,2,0,1:T(8,128)(2,1)}), bf16[1,6,1,128,1280]{4,3,2,0,1:T(8,128)(2,1)}) %all-gather.6.cloned.1.call-update) | async-done | bytes 1966096 | tf_op jit(solution)/shard_map/all_gather | solution.py:84
  89.6 4.5 copy.29
  94.1 5.3 reshape_transpose.9
  99.5 128.3 %all-gather.10.cloned.1.call-done = bf16[128,10,2432]{2,1,0:T(8,128)(2,1)} async-done(((bf16[1,10,2432]{2,1,0:T(8,128)(2,1)}), bf16[128,10,2432]{2,1,0:T(8,128)(2,1)}) %all-gather.10.cloned.1.call-update) | async-done | bytes 6225936 | tf_op jit(solution)/shard_map/all_gather | solution.py:78
  227.8 10.6 reshape.99
  238.5 6.5 convolution_convert_fusion.1
  246.5 115.3 %while.16 = (s32[]{:T(128)}, bf16[10,1,384,128]{2,3,1,0:T(8,128)(2,1)}, f32[10,1,768,128]{2,3,1,0:T(8,128)}, f32[10,1,768,128]{2,3,1,0:T(8,128)}, bf16[10,1,384,...) while((s32[]{:T(128)}, ...), condition=%wide.region_4.5_spmd, body=%wide.region_0.4_spmd.sunk | while | flops 461488128 | bytes 34821280 | solution.py:60
  249.4 2.4 fusion.57
  260.9 2.4 fusion.57
  284.0 2.4 fusion.57
  295.5 2.4 fusion.57
  307.0 2.4 fusion.57
  318.6 2.4 fusion.57
  330.1 2.4 fusion.57
  341.6 2.4 fusion.57
  361.9 7.5 fusion.13
  369.4 732.1 %all-reduce.2 = bf16[1280,2432]{1,0:T(8,128)(2,1)} all-reduce(f32[1280,2432]{1,0:T(8,128)} %fusion.13), channel_id=4, replica_groups=mesh['cam'=2,'band'=32,'obj'=4] {'band','obj'}, use_global_device_ids=true, to_apply=%region_7.8.clone | all-reduce | flops 3112960 | bytes 18677760
  1103.6 5.5 transpose_reshape.10
  1109.1 5.7 copy.39
  1114.8 5.4 transpose_reshape.11
  1120.3 5.7 copy.40
  1126.0 2.7 transpose_reshape.9
  1128.7 2.4 copy.41
  1132.8 55.5 %reduce-scatter.6.cloned.1.call-done = f32[1,3,1,128,1280]{4,3,2,0,1:T(8,128)} async-done(((f32[1,6,1,128,1280]{4,3,2,0,1:T(8,128)}), f32[1,3,1,128,1280]{4,3,2,0,1:T(8,128)}) %reduce-scatter.6.cloned.1.call-update) | async-done | bytes 1966096 | tf_op jit(solution)/shard_map/reduce_scatter | solution.py:89
  1188.3 2.6 convert_bitcast_fusion.1
  1190.9 57.9 %reduce-scatter.8.cloned.1.call-done = f32[1,3,1,128,1280]{4,3,2,0,1:T(8,128)} async-done(((f32[1,6,1,128,1280]{4,3,2,0,1:T(8,128)}), f32[1,3,1,128,1280]{4,3,2,0,1:T(8,128)}) %reduce-scatter.8.cloned.1.call-update) | async-done | bytes 1966096 | tf_op jit(solution)/shard_map/reduce_scatter | solution.py:90
  1248.8 2.6 convert_bitcast_fusion
  (172 shorter events, 105.8 us)
Async XLA Ops:
  7.2 231.3 %copy-start = (bf16[1,3,1,128,2432]{4,3,2,1,0:T(8,128)(2,1)S(1)}, bf16[1,3,1,128,2432]{4,3,2,1,0:T(8,128)(2,1)}, u32[]{:S(2)}) copy-start(bf16[1,3,1,128,2432]{4,3,2,1,0:T(8,128)(2,1)} %param.10) | copy-start | bytes 5603332
  7.2 43.0 %all-gather.8.cloned.1.call-start = ((), (), s32[]{:S(2)}) async-start(), calls=%async_computation.4 | async-start | bytes 2949120 | tf_op jit(solution)/shard_map/all_gather | solution.py:85
  7.9 81.7 %all-gather.6.cloned.1.call-start = ((), (), s32[]{:S(2)}) async-start(), calls=%async_computation.3 | async-start | bytes 2949120 | tf_op jit(solution)/shard_map/all_gather | solution.py:84
  8.7 219.1 %all-gather.10.cloned.1.call-start = ((), (), s32[]{:S(2)}) async-start(), calls=%async_computation.7 | async-start | bytes 10039296 | tf_op jit(solution)/shard_map/all_gather | solution.py:78
  13.9 4.6 copy-start.2
  13.9 1117.2 %reduce-scatter.10.cloned.1.call-start = ((), (), s32[]{:S(2)}) async-start(), calls=%async_computation.8 | async-start | bytes 933888
  251.8 2.4 copy-start.1
  263.3 2.4 copy-start.1
  274.8 2.4 copy-start.1
  286.3 2.4 copy-start.1
  297.9 2.4 copy-start.1
  309.4 2.4 copy-start.1
  321.0 2.4 copy-start.1
  332.5 2.4 copy-start.1
  344.0 2.4 copy-start.1
  355.6 2.4 copy-start.1
  1103.6 84.7 %reduce-scatter.6.cloned.1.call-start = ((), (), s32[]{:S(2)}) async-start(), calls=%async_computation.5 | async-start | bytes 5898240 | tf_op jit(solution)/shard_map/reduce_scatter | solution.py:89
  1114.8 134.0 %reduce-scatter.8.cloned.1.call-start = ((), (), s32[]{:S(2)}) async-start(), calls=%async_computation.6 | async-start | bytes 5898240 | tf_op jit(solution)/shard_map/reduce_scatter | solution.py:90
Sparse Core Ops, SparseCore 0:
  9.8 40.2 all-gather.7
  51.9 37.6 all-gather.5
  93.8 133.9 all-gather.9
  1103.7 24.0 reduce-scatter.9
  1130.2 58.1 reduce-scatter.5
  1190.7 58.1 reduce-scatter.7
where the time goes:
time: 1260 us
  blocking collectives  736 us (58%)
  waiting for transfers between devices  303 us (24%)
  local copies, waits for them, and re-layouts  113 us (9%)
  matrix products  80 us (6%)
  between operations  14.8 us (1%)
    unnamed x1, blocking collectives  732 us
    all_gather x1, waiting for transfers between devices, body(): lax.all_gather(full_cols, ('band', 'obj'), axis=0, tiled=True)  128 us
    reduce_scatter x1, waiting for transfers between devices, body(): lax.psum_scatter(partial_v, 'cam', scatter_dimension=1, tiled=True)  57.9 us
    reduce_scatter x1, waiting for transfers between devices, body(): lax.psum_scatter(partial_k, 'cam', scatter_dimension=1, tiled=True)  55.5 us
    all_gather x1, waiting for transfers between devices, body(): lax.all_gather(values, 'cam', axis=1, tiled=True)  30.4 us
    all_gather x1, waiting for transfers between devices, body(): lax.all_gather(keys, 'cam', axis=1, tiled=True)  29.6 us
    dynamic_slice x40, local copies, waits for them, and re-layouts, attend(): lax.map(pair_backward, (to_pairs(q_part), to_pairs(k_part), to_pairs(v_pa...  28.1 us
  transfers between devices with their start and end apart: 6, of which 5 were waited for; matrix products, arithmetic and copies ran while one was open for 5% of the time, Pallas kernels for 0%

commit v1 on v0

v1 whole, which is shorter than its diff:
```python
import functools
import math

import jax
import jax.numpy as jnp
from jax import lax
from jax.experimental import pallas as pl
from jax.experimental.pallas import tpu as pltpu
from jax.sharding import PartitionSpec as P

BF = jnp.bfloat16
F32 = jnp.float32
MESH = pl.DeviceIdType.MESH
NY, NZ = 4, 8
RING = NZ - 1
LAG = 10
RING_AT = 0
EXP_SCALE = 0.125 / math.log(2.0)


def nn(a, b):
    return lax.dot_general(a, b, (((1,), (0,)), ((), ())), preferred_element_type=F32)


def nt(a, b):
    return lax.dot_general(a, b, (((1,), (1,)), ((), ())), preferred_element_type=F32)


def picker(rows, cols, row_step, col_step, width):
    r = lax.broadcasted_iota(jnp.int32, (rows, cols), 0)
    c = lax.broadcasted_iota(jnp.int32, (rows, cols), 1)
    pick = jnp.zeros((rows, cols), F32)
    for b in range(4):
        k = r - row_step * b
        hit = (k >= 0) & (k < width) & (c - col_step * b == k)
        pick = pick + jnp.where(hit, 1.0, 0.0).astype(F32)
    return pick.astype(BF)


def halves(x, axis):
    index = lax.broadcasted_iota(jnp.int32, x.shape, axis)
    first = jnp.where(index < x.shape[axis] // 2, x, 0.0)
    return first.astype(BF), (x - first).astype(BF)


def kernel(scale, q_hbm, k_hbm, v_hbm, d_hbm, w_ref, gq_hbm, gk_hbm, gv_hbm, gwo_ref,
           qb, kb, vb, dfull, dcat, doth, wpad, wx, wy, wown, woth, att, lse, osum,
           dks, dkr, dko, gq_st, gk_st, gv_st, gacc, rss, rsr, gys, gyr, gxs, gxr,
           q_ld, k_ld, v_ld, d_ld, wx_s, wx_r, wy_s, wy_r, zr_s, zr_r, zl_s, zl_r,
           oc_s, oc_r, k_s, k_r, v_s, v_r, dx_s, dx_r, at_s, at_r, dk_s, dk_r, dv_s, dv_r,
           rr_s, rr_r, rl_s, rl_r, gy_s, gy_r, gx_s, gx_r, gq_o, gk_o, gv_o):
    pairs, toks = qb.shape[0], qb.shape[1]
    cols = wpad.shape[1]
    blk = wown.shape[0] // NZ
    half = blk // 2
    cam, band, obj = lax.axis_index("cam"), lax.axis_index("band"), lax.axis_index("obj")
    z, y = band // NY, band % NY
    xh, core = obj // 2, obj % 2
    x = xh * 2 + cam
    base = (blk * z + half) // 128

    def dev(cam_=None, band_=None, obj_=None):
        return {
            "cam": cam if cam_ is None else cam_,
            "band": band if band_ is None else band_,
            "obj": obj if obj_ is None else obj_,
        }

    def at_z(shift):
        return dev(band_=lax.rem(z + shift + NZ, NZ) * NY + y)

    def at_y(shift):
        return dev(band_=z * NY + lax.rem(y + shift, NY))

    cam_peer = dev(cam_=1 - cam)
    core_peer = dev(obj_=xh * 2 + 1 - core)
    z_up, z_down = at_z(1), at_z(-1)

    def remote(src, dst, send, recv, device):
        return pltpu.make_async_remote_copy(
            src_ref=src, dst_ref=dst, send_sem=send, recv_sem=recv, device_id=device,
            device_id_type=MESH)

    def order(i):
        step = (i + 1) // 2
        sign = 2 * (i % 2) - 1
        return lax.rem(base + sign * step + pairs, pairs)

    def lanes(i):
        return pl.ds(pl.multiple_of(order(i) * 128, 128), 128)

    def load_q(i):
        return pltpu.make_async_copy(q_hbm.at[:, lanes(i)], qb.at[i], q_ld.at[i])

    def load_k(i):
        return pltpu.make_async_copy(k_hbm.at[:, lanes(i)], kb.at[i, 0], k_ld.at[i])

    def load_v(i):
        return pltpu.make_async_copy(v_hbm.at[:, lanes(i)], vb.at[i, 0], v_ld.at[i])

    def send_k(i):
        return remote(k_hbm.at[:, lanes(i)], kb.at[i, 1], k_s.at[i], k_r.at[i], cam_peer)

    def send_v(i):
        return remote(v_hbm.at[:, lanes(i)], vb.at[i, 1], v_s.at[i], v_r.at[i], cam_peer)

    load_d = pltpu.make_async_copy(d_hbm, dfull, d_ld)
    load_d.start()
    wpad[...] = jnp.zeros_like(wpad)
    wpad[0:10, :] = w_ref[...]

    @pl.loop(0, pairs)
    def _(i):
        load_q(i).start()
        load_k(i).start()
        load_v(i).start()

    barrier = pltpu.get_barrier_semaphore()
    peers = [dev(cam_=lax.rem(cam + a, 2), obj_=lax.rem(obj + b, 4))
             for a in range(2) for b in range(4) if a + b > 0]
    peers += [at_y(s) for s in range(1, NY)] + [z_up, z_down]
    for peer in peers:
        pl.semaphore_signal(barrier, inc=1, device_id=peer, device_id_type=MESH)
    pl.semaphore_wait(barrier, len(peers))

    def w_to(t):
        return remote(wpad, wx.at[obj], wx_s.at[t], wx_r.at[obj],
                      dev(cam_=t % 2, obj_=(t // 2) * 2 + cam))

    own_target = core == cam
    for t in range(4):
        mine = own_target & (x == t)

        @pl.when(jnp.logical_not(mine))
        def _():
            w_to(t).start()

    @pl.when(own_target)
    def _():
        pltpu.make_async_copy(wpad, wx.at[obj], wx_r.at[obj]).start()

    @pl.loop(0, pairs)
    def _(i):
        send_k(i).start()
        send_v(i).start()

    load_d.wait()
    low, high = dfull[:, 0:cols], dfull[:, cols:2 * cols]

    @pl.when(core == 0)
    def _():
        dcat[0:toks, :] = low
        doth[...] = high

    @pl.when(core == 1)
    def _():
        dcat[0:toks, :] = high
        doth[...] = low

    d_swap = remote(doth, dcat.at[pl.ds(toks, toks)], dx_s, dx_r, core_peer)
    d_swap.start()

    for o in range(4):
        pltpu.make_async_copy(wpad, wx.at[o], wx_r.at[o]).wait()
    joined = nn(picker(48, 64, 10, 16, 10), wx[...].reshape(64, cols)).astype(BF)
    wy[y] = joined

    def y_copy(s):
        return remote(wy.at[y], wy.at[y], wy_s.at[s], wy_r.at[s], at_y(s))

    for s in range(1, NY):
        y_copy(s).start()
    for s in range(1, NY):
        y_copy(s).wait_recv()

    def block_rows(b, size=None, off=0):
        return pl.ds(pl.multiple_of(b * blk + off, 16), blk if size is None else size)

    wown[block_rows(z), :] = nn(picker(blk, 4 * 48, 40, 48, 40), wy[...].reshape(4 * 48, cols)).astype(BF)

    def up_copy(h, back):
        b = lax.rem(z - h // 2 - back + NZ, NZ)
        rows = block_rows(b, half, (h % 2) * half)
        return remote(wown.at[rows], wown.at[rows], zr_s.at[h], zr_r.at[h], z_up)

    def down_copy(h, back):
        b = lax.rem(z + h // 2 + back, NZ)
        rows = block_rows(b, half, (1 - h % 2) * half)
        return remote(wown.at[rows], wown.at[rows], zl_s.at[h], zl_r.at[h], z_down)

    def cross(h, up):
        b = lax.rem(z - h // 2 - 1 + NZ, NZ) if up else lax.rem(z + h // 2 + 1, NZ)
        j = h % 2 if up else 1 - h % 2
        rows = block_rows(b, half, j * half)
        n = 2 * h + (0 if up else 1)
        return remote(wown.at[rows], woth.at[rows], oc_s.at[n], oc_r.at[n], core_peer)

    own_rows = block_rows(z)
    cross_own = remote(wown.at[own_rows], woth.at[own_rows], oc_s.at[2 * RING], oc_r.at[2 * RING], core_peer)
    for h in range(2):
        up_copy(h, 0).start()
        down_copy(h, 0).start()
    cross_own.start()

    def ring(h):
        up_copy(h, 1).wait_recv()

        @pl.when(h + 2 < RING)
        def _():
            up_copy(h + 2, 0).start()

        down_copy(h, 1).wait_recv()

        @pl.when(h + 2 < RING)
        def _():
            down_copy(h + 2, 0).start()

        cross(h, True).start()
        cross(h, False).start()

    def split_q(i):
        first, second = halves(qb[i].astype(F32), 1)
        return jnp.concatenate([first, second], axis=0)

    def swap_att(i):
        rows = pl.ds(pl.multiple_of(order(i) * 128, 128), 128)
        return remote(att.at[rows, pl.ds(0, toks)], att.at[rows, pl.ds(toks, toks)],
                      at_s.at[i], at_r.at[i], core_peer)

    part = 2 * toks // 3

    def forward(i):
        load_q(i).wait()
        load_k(i).wait()
        load_v(i).wait()
        send_k(i).wait_recv()
        send_v(i).wait_recv()
        kk = kb[i].reshape(2 * toks, 128)
        vt = vb[i].reshape(2 * toks, 128).T
        qm = split_q(i)
        for n in range(3):
            s = nt(kk, qm[n * part:(n + 1) * part])
            top = jnp.max(s, axis=0, keepdims=True)
            e = jnp.exp2((s - top) * EXP_SCALE)
            total = jnp.sum(e, axis=0, keepdims=True)
            osum[:, n * part:(n + 1) * part] = nn(vt, e.astype(BF)) * (1.0 / total)
            lse[i, :, n * part:(n + 1) * part] = top * EXP_SCALE + jnp.log2(total)
        rows = pl.ds(pl.multiple_of(order(i) * 128, 128), 128)
        both = jnp.concatenate([osum[0:64, 0:toks], osum[64:128, toks:2 * toks]], axis=0)
        att[rows, 0:toks] = both.astype(BF)
        swap_att(i).start()

    def give_k(i):
        return remote(dks.at[i, 0], dkr.at[i, 0], dk_s.at[i], dk_r.at[i], cam_peer)

    def give_v(i):
        return remote(dks.at[i, 1], dkr.at[i, 1], dv_s.at[i], dv_r.at[i], cam_peer)

    def put_q(i):
        return pltpu.make_async_copy(gq_st.at[i], gq_hbm.at[:, lanes(i)], gq_o.at[i])

    def put_k(i):
        return pltpu.make_async_copy(gk_st.at[i], gk_hbm.at[:, lanes(i)], gk_o.at[i])

    def put_v(i):
        return pltpu.make_async_copy(gv_st.at[i], gv_hbm.at[:, lanes(i)], gv_o.at[i])

    def backward(i):
        rows = pl.ds(pl.multiple_of(order(i) * 128, 128), 128)
        da = nt(wown[rows, :], dcat[0:toks, :]) + nt(woth[rows, :], doth[...])
        da = da.astype(BF).astype(F32)
        prod = da * att[rows, 0:toks].astype(F32)
        delta = jnp.concatenate([jnp.sum(prod[0:64], axis=0, keepdims=True),
                                 jnp.sum(prod[64:128], axis=0, keepdims=True)], axis=1)
        dm = jnp.concatenate(halves(da, 0), axis=1)
        kk = kb[i].reshape(2 * toks, 128)
        vv = vb[i].reshape(2 * toks, 128)
        kt = kk.T
        qm = split_q(i)
        dk = dv = None
        for n in range(3):
            at = slice(n * part, (n + 1) * part)
            s = nt(kk, qm[at])
            p = jnp.exp2(s * EXP_SCALE - lse[i, :, at])
            dp = nn(vv, dm[:, at])
            ds = (p * (dp - delta[:, at])).astype(BF)
            dv_n = nt(p.astype(BF), dm[:, at])
            dk_n = nn(ds, qm[at])
            dv = dv_n if dv is None else dv + dv_n
            dk = dk_n if dk is None else dk + dk_n
            osum[:, at] = nn(kt, ds)
        dk = dk * 0.125
        dks[i, 0] = dk[toks:].astype(BF)
        dks[i, 1] = dv[toks:].astype(BF)
        give_k(i).start()
        give_v(i).start()
        dko[i, 0] = dk[:toks]
        dko[i, 1] = dv[:toks]
        both = jnp.concatenate([osum[0:64, 0:toks], osum[64:128, toks:2 * toks]], axis=0)
        gq_st[i] = (both.T * 0.125).astype(BF)
        put_q(i).start()

    def finish(i):
        give_k(i).wait_recv()
        gk_st[i] = (dko[i, 0] + dkr[i, 0].astype(F32)).astype(BF)
        put_k(i).start()
        give_v(i).wait_recv()
        gv_st[i] = (dko[i, 1] + dkr[i, 1].astype(F32)).astype(BF)
        put_v(i).start()

    def sum_up(s):
        return remote(rss.at[s, 0], rsr.at[s, 0], rr_s.at[s], rr_r.at[s], z_up)

    def sum_down(s):
        return remote(rss.at[s, 1], rsr.at[s, 1], rl_s.at[s], rl_r.at[s], z_down)

    def sum_step(s):
        owner_up = lax.rem(z - 1 - s + 2 * NZ, NZ)
        owner_down = lax.rem(z + 1 + s, NZ)
        rows = jnp.concatenate([att[block_rows(owner_up, half), :],
                                att[block_rows(owner_down, half, half), :]], axis=0)
        gacc[...] = nn(rows, dcat[...])

        @pl.when(s > 0)
        def _():
            sum_up(s - 1).wait_recv()
            gacc[0:half, :] = gacc[0:half, :] + rsr[s - 1, 0].astype(F32)
            sum_down(s - 1).wait_recv()
            gacc[half:blk, :] = gacc[half:blk, :] + rsr[s - 1, 1].astype(F32)

        @pl.when(s < RING)
        def _():
            rss[s, 0] = gacc[0:half, :].astype(BF)
            sum_up(s).start()
            rss[s, 1] = gacc[half:blk, :].astype(BF)
            sum_down(s).start()

    @pl.loop(0, pairs + LAG)
    def _(t):
        h = t - RING_AT

        @pl.when((h >= 0) & (h < RING))
        def _():
            ring(h)

        @pl.when(t < pairs)
        def _():
            forward(t)

        @pl.when(t == pairs - 1)
        def _():
            d_swap.wait_recv()
            cross_own.wait_recv()
            for n in range(RING):
                cross(n, True).wait_recv()
                cross(n, False).wait_recv()

            @pl.loop(0, pairs)
            def _(i):
                swap_att(i).wait_recv()

        @pl.when(t >= LAG)
        def _():
            backward(t - LAG)

        s = t - pairs

        @pl.when((s >= 0) & (s < NZ))
        def _():
            sum_step(s)

    def sum_y(s):
        return remote(gys.at[lax.rem(y + s, NY)], gyr.at[s], gy_s.at[s], gy_r.at[s], at_y(s))

    gys[...] = nn(picker(4 * 48, blk, 48, 40, 40), gacc[...].astype(BF)).astype(BF).reshape(4, 48, cols)
    for s in range(1, NY):
        sum_y(s).start()
    summed = gys[y].astype(F32)
    for s in range(1, NY):
        sum_y(s).wait_recv()
        summed = summed + gyr[s].astype(F32)
    gxs[...] = nn(picker(64, 48, 16, 10, 10), summed.astype(BF)).astype(BF).reshape(4, 16, cols)

    def sum_x(o):
        return remote(gxs.at[o], gxr.at[x], gx_s.at[o], gx_r.at[x], dev(cam_=core, obj_=o))

    for o in range(4):
        mine = own_target & (obj == o)

        @pl.when(jnp.logical_not(mine))
        def _():
            sum_x(o).start()

        @pl.when(mine)
        def _():
            pltpu.make_async_copy(gxs.at[o], gxr.at[x], gx_r.at[x]).start()

    @pl.loop(0, pairs)
    def _(i):
        finish(i)

    for o in range(4):
        pltpu.make_async_copy(gxs.at[o], gxr.at[o], gx_r.at[o]).wait()
    total = gxr[0].astype(F32) + gxr[1].astype(F32) + gxr[2].astype(F32) + gxr[3].astype(F32)
    gwo_ref[...] = total[0:10, :] * scale

    for t in range(4):
        @pl.when(jnp.logical_not(own_target & (x == t)))
        def _():
            w_to(t).wait_send()

        @pl.when(jnp.logical_not(own_target & (obj == t)))
        def _():
            sum_x(t).wait_send()

    for s in range(1, NY):
        y_copy(s).wait_send()
        sum_y(s).wait_send()
    d_swap.wait_send()
    cross_own.wait_send()

    @pl.loop(0, RING)
    def _(h):
        up_copy(h, 0).wait_send()
        down_copy(h, 0).wait_send()
        cross(h, True).wait_send()
        cross(h, False).wait_send()
        sum_up(h).wait_send()
        sum_down(h).wait_send()

    @pl.loop(0, pairs)
    def _(i):
        send_k(i).wait_send()
        send_v(i).wait_send()
        swap_att(i).wait_send()
        give_k(i).wait_send()
        give_v(i).wait_send()
        put_q(i).wait()
        put_k(i).wait()
        put_v(i).wait()


def body(queries, keys, values, d_out, w_out):
    shape = queries.shape
    width, model = queries.shape[4], d_out.shape[4]
    toks = queries.shape[1] * queries.shape[2] * queries.shape[3]
    tokens = toks * lax.axis_size("cam") * lax.axis_size("band") * lax.axis_size("obj")
    scale = float(tokens) ** -0.5
    pairs = width // 128
    cols = w_out.shape[1]
    blk = width // NZ
    dma = lambda *n: pltpu.SemaphoreType.DMA(n)
    flat = lambda a: a.reshape(toks, a.shape[4])
    any_ = pl.BlockSpec(memory_space=pl.ANY)
    vmem = pl.BlockSpec(memory_space=pltpu.VMEM)
    grad = jax.ShapeDtypeStruct((toks, width), BF)
    scratch = [
        pltpu.VMEM((pairs, toks, 128), BF),
        pltpu.VMEM((pairs, 2, toks, 128), BF),
        pltpu.VMEM((pairs, 2, toks, 128), BF),
        pltpu.VMEM((toks, model), BF),
        pltpu.VMEM((2 * toks, cols), BF),
        pltpu.VMEM((toks, cols), BF),
        pltpu.VMEM((16, cols), BF),
        pltpu.VMEM((4, 16, cols), BF),
        pltpu.VMEM((4, 48, cols), BF),
        pltpu.VMEM((width, cols), BF),
        pltpu.VMEM((width, cols), BF),
        pltpu.VMEM((width, 2 * toks), BF),
        pltpu.VMEM((pairs, 1, 2 * toks), F32),
        pltpu.VMEM((128, 2 * toks), F32),
        pltpu.VMEM((pairs, 2, toks, 128), BF),
        pltpu.VMEM((pairs, 2, toks, 128), BF),
        pltpu.VMEM((pairs, 2, toks, 128), F32),
        pltpu.VMEM((pairs, toks, 128), BF),
        pltpu.VMEM((pairs, toks, 128), BF),
        pltpu.VMEM((pairs, toks, 128), BF),
        pltpu.VMEM((blk, cols), F32),
        pltpu.VMEM((RING, 2, blk // 2, cols), BF),
        pltpu.VMEM((RING, 2, blk // 2, cols), BF),
        pltpu.VMEM((4, 48, cols), BF),
        pltpu.VMEM((4, 48, cols), BF),
        pltpu.VMEM((4, 16, cols), BF),
        pltpu.VMEM((4, 16, cols), BF),
        dma(pairs), dma(pairs), dma(pairs), pltpu.SemaphoreType.DMA,
        dma(4), dma(4), dma(4), dma(4), dma(RING), dma(RING), dma(RING), dma(RING),
        dma(2 * RING + 1), dma(2 * RING + 1), dma(pairs), dma(pairs), dma(pairs), dma(pairs),
        pltpu.SemaphoreType.DMA, pltpu.SemaphoreType.DMA, dma(pairs), dma(pairs),
        dma(pairs), dma(pairs), dma(pairs), dma(pairs),
        dma(RING), dma(RING), dma(RING), dma(RING), dma(4), dma(4), dma(4), dma(4),
        dma(pairs), dma(pairs), dma(pairs),
    ]
    gq, gk, gv, gwo = pl.pallas_call(
        functools.partial(kernel, scale),
        out_shape=(grad, grad, grad, jax.ShapeDtypeStruct(w_out.shape, F32)),
        in_specs=[any_] * 4 + [vmem],
        out_specs=(any_, any_, any_, vmem),
        scratch_shapes=scratch,
        compiler_params=pltpu.CompilerParams(
            collective_id=0, has_side_effects=True, vmem_limit_bytes=64 * 1024 * 1024 - 65536),
        name="row_attention_backward",
    )(flat(queries), flat(keys), flat(values), flat(d_out), w_out)
    return gq.reshape(shape), gk.reshape(shape), gv.reshape(shape), gwo


def solution(mesh):
    act = P("obj", "cam", "band", None, None)
    proj = P(("band", "obj"), "cam")
    return jax.shard_map(
        body,
        mesh=mesh,
        in_specs=(act, act, act, act, proj),
        out_specs=(act, act, act, proj),
        check_vma=False,
    )
```

time: 1260 us -> 136 us (0.11)
  blocking collectives: 736 us -> 0 us
  waiting for transfers between devices: 303 us -> 0 us
  Pallas kernels: 0 us -> 130 us
  local copies, waits for them, and re-layouts: 113 us -> 4.88 us
  matrix products: 80 us -> 0 us
  between operations: 14.8 us -> 0.66 us
    unnamed x1 -> x0, blocking collectives: 732 us -> none
    all_gather x3 -> x0, waiting for transfers between devices: 188 us -> none  [the longest x1 128 us: body(): lax.all_gather(full_cols, ('band', 'obj'), axis=0, tiled=True)]
    pallas_call x0 -> x1, Pallas kernels: none -> 130 us  [body(): pl.pallas_call(functools.partial(kernel, scale), out_shape=(grad, grad, g...]
    reduce_scatter x2 -> x0, waiting for transfers between devices: 113 us -> none  [the longest x1 57.9 us: body(): lax.psum_scatter(partial_v, 'cam', scatter_dimension=1, tiled=True)]
    dot_general x52 -> x0, matrix products: 56.1 us -> none  [the longest x10 23.6 us: pair_backward(): jnp.einsum('ghqk,gkhe->gqhe', probs_b, v_heads, preferred_element_type=jn...]
    another operation x8 -> x0, local copies, waits for them, and re-layouts: 37.2 us -> none  [the longest x5 24.9 us: from_pairs(): return merged.transpose(0, 2, 1, 3, 4)]
    dynamic_slice x40 -> x0, local copies, waits for them, and re-layouts: 28.1 us -> none  [attend(): lax.map(pair_backward, (to_pairs(q_part), to_pairs(k_part), to_pairs(v_pa...]
    sub x10 -> x0, matrix products: 23.9 us -> none  [pair_backward(): expd = jnp.exp(scores - top)]
  transfers between devices with their start and end apart: 6 -> 0, of which waited for: 5 -> 0; matrix products, arithmetic and copies ran while one was open for 5% -> 0% of each run, Pallas kernels for 0% -> 0%
where the time goes in v1:
time: 136 us; the launch traced here: 135 us
  Pallas kernels  130 us (96%)
  local copies, waits for them, and re-layouts  4.88 us (4%)
    pallas_call x1, Pallas kernels, body(): pl.pallas_call(functools.partial(kernel, scale), out_shape=(grad, grad, g...  130 us
    unnamed x10, local copies, waits for them, and re-layouts  4.88 us

profile of v1, /device:TPU:1, one launch (start us, length us, event | category | flops | bytes accessed | tf_op | source)
XLA Modules:
  0.0 135.4 jit_solution(123042372364662822)
XLA Ops:
  0.6 129.9 %row_attention_backward.1 = (bf16[384,1280]{1,0:T(8,128)(2,1)}, bf16[384,1280]{1,0:T(8,128)(2,1)}, bf16[384,1280]{1,0:T(8,128)(2,1)}, f32[10,1216]{1,0:T(8,128)}) custom-call(bf16[384,1280]{1,0:T(8,128)(2,1)} %bitcast.14, bf16[384,1280]{1,0:T(8,128)(2,1)} %bitcast.15, bf16[384,1280]{1,0:T(8,128)(2,1)} %bitcast.16, bf16[384,2432]{1,0:T(8,128)(2,1)} %bitcast.13, ...), custom_call_target="tpu_custom_call" | custom-call | tf_op jit(solution)/shard_map/row_attention_backward/pallas_call | solution.py:493
  130.5 0.0 copy-start.1
  130.5 0.0 copy-start
  130.5 2.3 %copy.16 = bf16[1,3,1,128,1280]{4,3,2,1,0:T(8,128)(2,1)} copy(bf16[1,3,1,128,1280]{4,3,2,1,0:T(8,128)(2,1)} %bitcast.19) | data formatting | bytes 1966080
  132.9 0.0 copy-done.1
  132.9 0.0 copy-start.2
  132.9 0.9 copy.17
  133.8 0.0 copy-done
  133.8 0.9 copy.18
  134.8 0.0 copy-done.2
  134.8 0.6 copy.19
Async XLA Ops:
  130.5 2.4 %copy-start.1 = (bf16[384,1280]{1,0:T(8,128)(2,1)S(1)}, bf16[384,1280]{1,0:T(8,128)(2,1)}, u32[]{:S(2)}) copy-start(bf16[384,1280]{1,0:T(8,128)(2,1)} %get-tuple-element.9) | copy-start | bytes 2949124
  130.5 3.3 %copy-start = (bf16[384,1280]{1,0:T(8,128)(2,1)S(1)}, bf16[384,1280]{1,0:T(8,128)(2,1)}, u32[]{:S(2)}) copy-start(bf16[384,1280]{1,0:T(8,128)(2,1)} %get-tuple-element.10) | copy-start | bytes 2949124
  132.9 1.9 %copy-start.2 = (f32[10,1216]{1,0:T(8,128)S(1)}, f32[10,1216]{1,0:T(8,128)}, u32[]{:S(2)}) copy-start(f32[10,1216]{1,0:T(8,128)} %get-tuple-element.23) | copy-start | bytes 145924

commit v2 on v1

--- a/solution.py
+++ b/solution.py
@@ -13,8 +13,9 @@
 MESH = pl.DeviceIdType.MESH
 NY, NZ = 4, 8
 RING = NZ - 1
-LAG = 10
-RING_AT = 0
+LAG = 6
+RING_AT = 4
+SUBS = ((0, 48), (48, 32))
 EXP_SCALE = 0.125 / math.log(2.0)
 
 
@@ -144,6 +145,18 @@
         send_k(i).start()
         send_v(i).start()
 
+    join_x = picker(48, 64, 10, 16, 10)
+    for o in range(4):
+        pltpu.make_async_copy(wpad, wx.at[o], wx_r.at[o]).wait()
+    joined = nn(join_x, wx[...].reshape(64, cols)).astype(BF)
+    wy[y] = joined
+
+    def y_copy(s):
+        return remote(wy.at[y], wy.at[y], wy_s.at[s], wy_r.at[s], at_y(s))
+
+    for s in range(1, NY):
+        y_copy(s).start()
+
     load_d.wait()
     low, high = dfull[:, 0:cols], dfull[:, cols:2 * cols]
 
@@ -160,23 +173,14 @@
     d_swap = remote(doth, dcat.at[pl.ds(toks, toks)], dx_s, dx_r, core_peer)
     d_swap.start()
 
-    for o in range(4):
-        pltpu.make_async_copy(wpad, wx.at[o], wx_r.at[o]).wait()
-    joined = nn(picker(48, 64, 10, 16, 10), wx[...].reshape(64, cols)).astype(BF)
-    wy[y] = joined
-
-    def y_copy(s):
-        return remote(wy.at[y], wy.at[y], wy_s.at[s], wy_r.at[s], at_y(s))
-
-    for s in range(1, NY):
-        y_copy(s).start()
+    join_y = picker(blk, 4 * 48, 40, 48, 40)
     for s in range(1, NY):
         y_copy(s).wait_recv()
 
     def block_rows(b, size=None, off=0):
         return pl.ds(pl.multiple_of(b * blk + off, 16), blk if size is None else size)
 
-    wown[block_rows(z), :] = nn(picker(blk, 4 * 48, 40, 48, 40), wy[...].reshape(4 * 48, cols)).astype(BF)
+    wown[block_rows(z), :] = nn(join_y, wy[...].reshape(4 * 48, cols)).astype(BF)
 
     def up_copy(h, back):
         b = lax.rem(z - h // 2 - back + NZ, NZ)
@@ -308,66 +312,80 @@
         gv_st[i] = (dko[i, 1] + dkr[i, 1].astype(F32)).astype(BF)
         put_v(i).start()
 
-    def sum_up(s):
-        return remote(rss.at[s, 0], rsr.at[s, 0], rr_s.at[s], rr_r.at[s], z_up)
-
-    def sum_down(s):
-        return remote(rss.at[s, 1], rsr.at[s, 1], rl_s.at[s], rl_r.at[s], z_down)
-
-    def sum_step(s):
+    def sum_up(s, sub):
+        at = pl.ds(*SUBS[sub])
+        return remote(rss.at[s, 0, at], rsr.at[s, 0, at], rr_s.at[s, sub], rr_r.at[s, sub], z_up)
+
+    def sum_down(s, sub):
+        at = pl.ds(*SUBS[sub])
+        return remote(rss.at[s, 1, at], rsr.at[s, 1, at], rl_s.at[s, sub], rl_r.at[s, sub], z_down)
+
+    def own_term(s):
         owner_up = lax.rem(z - 1 - s + 2 * NZ, NZ)
         owner_down = lax.rem(z + 1 + s, NZ)
         rows = jnp.concatenate([att[block_rows(owner_up, half), :],
                                 att[block_rows(owner_down, half, half), :]], axis=0)
         gacc[...] = nn(rows, dcat[...])
 
-        @pl.when(s > 0)
-        def _():
-            sum_up(s - 1).wait_recv()
-            gacc[0:half, :] = gacc[0:half, :] + rsr[s - 1, 0].astype(F32)
-            sum_down(s - 1).wait_recv()
-            gacc[half:blk, :] = gacc[half:blk, :] + rsr[s - 1, 1].astype(F32)
+    def sum_step(s):
+        for sub, (off, size) in enumerate(SUBS):
+            for way, copy in enumerate((sum_up, sum_down)):
+                at = slice(way * half + off, way * half + off + size)
+
+                @pl.when(s > 0)
+                def _():
+                    copy(s - 1, sub).wait_recv()
+                    gacc[at, :] = gacc[at, :] + rsr[s - 1, way, off:off + size].astype(F32)
+
+                @pl.when(s < RING)
+                def _():
+                    rss[s, way, off:off + size] = gacc[at, :].astype(BF)
+                    copy(s, sub).start()
 
         @pl.when(s < RING)
         def _():
-            rss[s, 0] = gacc[0:half, :].astype(BF)
-            sum_up(s).start()
-            rss[s, 1] = gacc[half:blk, :].astype(BF)
-            sum_down(s).start()
-
-    @pl.loop(0, pairs + LAG)
+            own_term(s + 1)
+
+    @pl.loop(0, pairs + NZ)
     def _(t):
+        @pl.when(t < pairs)
+        def _():
+            forward(t)
+
         h = t - RING_AT
 
+        @pl.when(h == 0)
+        def _():
+            cross_own.wait_recv()
+
+        @pl.when((h >= 1) & (h <= RING))
+        def _():
+            cross(h - 1, True).wait_recv()
+            cross(h - 1, False).wait_recv()
+
         @pl.when((h >= 0) & (h < RING))
         def _():
             ring(h)
 
-        @pl.when(t < pairs)
-        def _():
-            forward(t)
-
-        @pl.when(t == pairs - 1)
+        s = t - pairs
+
+        @pl.when(s == 0)
         def _():
             d_swap.wait_recv()
-            cross_own.wait_recv()
-            for n in range(RING):
-                cross(n, True).wait_recv()
-                cross(n, False).wait_recv()
 
             @pl.loop(0, pairs)
             def _(i):
                 swap_att(i).wait_recv()
 
-        @pl.when(t >= LAG)
+            own_term(0)
+
+        @pl.when(s >= 0)
+        def _():
+            sum_step(s)
+
+        @pl.when((t >= LAG) & (t < LAG + pairs))
         def _():
             backward(t - LAG)
-
-        s = t - pairs
-
-        @pl.when((s >= 0) & (s < NZ))
-        def _():
-            sum_step(s)
 
     def sum_y(s):
         return remote(gys.at[lax.rem(y + s, NY)], gyr.at[s], gy_s.at[s], gy_r.at[s], at_y(s))
@@ -375,6 +393,11 @@
     gys[...] = nn(picker(4 * 48, blk, 48, 40, 40), gacc[...].astype(BF)).astype(BF).reshape(4, 48, cols)
     for s in range(1, NY):
         sum_y(s).start()
+
+    @pl.loop(0, pairs - 3)
+    def _(i):
+        finish(i)
+
     summed = gys[y].astype(F32)
     for s in range(1, NY):
         sum_y(s).wait_recv()
@@ -395,7 +418,7 @@
         def _():
             pltpu.make_async_copy(gxs.at[o], gxr.at[x], gx_r.at[x]).start()
 
-    @pl.loop(0, pairs)
+    @pl.loop(pairs - 3, pairs)
     def _(i):
         finish(i)
 
@@ -425,8 +448,9 @@
         down_copy(h, 0).wait_send()
         cross(h, True).wait_send()
         cross(h, False).wait_send()
-        sum_up(h).wait_send()
-        sum_down(h).wait_send()
+        for sub in range(len(SUBS)):
+            sum_up(h, sub).wait_send()
+            sum_down(h, sub).wait_send()
 
     @pl.loop(0, pairs)
     def _(i):
@@ -487,7 +511,7 @@
         dma(2 * RING + 1), dma(2 * RING + 1), dma(pairs), dma(pairs), dma(pairs), dma(pairs),
         pltpu.SemaphoreType.DMA, pltpu.SemaphoreType.DMA, dma(pairs), dma(pairs),
         dma(pairs), dma(pairs), dma(pairs), dma(pairs),
-        dma(RING), dma(RING), dma(RING), dma(RING), dma(4), dma(4), dma(4), dma(4),
+        dma(RING, 2), dma(RING, 2), dma(RING, 2), dma(RING, 2), dma(4), dma(4), dma(4), dma(4),
         dma(pairs), dma(pairs), dma(pairs),
     ]
     gq, gk, gv, gwo = pl.pallas_call(

time: 136 us -> 120 us (0.88)
  Pallas kernels: 130 us -> 114 us
    pallas_call x1, Pallas kernels: 130 us -> 114 us  [body(): pl.pallas_call(functools.partial(kernel, scale), out_shape=(grad, grad, g...]
where the time goes in v2:
time: 120 us
  Pallas kernels  114 us (95%)
  local copies, waits for them, and re-layouts  4.88 us (4%)
    pallas_call x1, Pallas kernels, body(): pl.pallas_call(functools.partial(kernel, scale), out_shape=(grad, grad, g...  114 us
    unnamed x10, local copies, waits for them, and re-layouts  4.88 us

profile of v2, /device:TPU:1, one launch (start us, length us, event | category | flops | bytes accessed | tf_op | source)
XLA Modules:
  0.0 119.8 jit_solution(4082623886070145218)
XLA Ops:
  0.6 114.3 %row_attention_backward.1 = (bf16[384,1280]{1,0:T(8,128)(2,1)}, bf16[384,1280]{1,0:T(8,128)(2,1)}, bf16[384,1280]{1,0:T(8,128)(2,1)}, f32[10,1216]{1,0:T(8,128)}) custom-call(bf16[384,1280]{1,0:T(8,128)(2,1)} %bitcast.14, bf16[384,1280]{1,0:T(8,128)(2,1)} %bitcast.15, bf16[384,1280]{1,0:T(8,128)(2,1)} %bitcast.16, bf16[384,2432]{1,0:T(8,128)(2,1)} %bitcast.13, ...), custom_call_target="tpu_custom_call" | custom-call | tf_op jit(solution)/shard_map/row_attention_backward/pallas_call | solution.py:517
  114.9 0.0 copy-start.1
  114.9 0.0 copy-start
  114.9 2.3 %copy.16 = bf16[1,3,1,128,1280]{4,3,2,1,0:T(8,128)(2,1)} copy(bf16[1,3,1,128,1280]{4,3,2,1,0:T(8,128)(2,1)} %bitcast.19) | data formatting | bytes 1966080
  117.3 0.0 copy-done.1
  117.3 0.0 copy-start.2
  117.3 0.9 copy.17
  118.2 0.0 copy-done
  118.2 0.9 copy.18
  119.2 0.0 copy-done.2
  119.2 0.6 copy.19
Async XLA Ops:
  114.9 2.4 %copy-start.1 = (bf16[384,1280]{1,0:T(8,128)(2,1)S(1)}, bf16[384,1280]{1,0:T(8,128)(2,1)}, u32[]{:S(2)}) copy-start(bf16[384,1280]{1,0:T(8,128)(2,1)} %get-tuple-element.9) | copy-start | bytes 2949124
  114.9 3.3 %copy-start = (bf16[384,1280]{1,0:T(8,128)(2,1)S(1)}, bf16[384,1280]{1,0:T(8,128)(2,1)}, u32[]{:S(2)}) copy-start(bf16[384,1280]{1,0:T(8,128)(2,1)} %get-tuple-element.10) | copy-start | bytes 2949124
  117.3 1.9 %copy-start.2 = (f32[10,1216]{1,0:T(8,128)S(1)}, f32[10,1216]{1,0:T(8,128)}, u32[]{:S(2)}) copy-start(f32[10,1216]{1,0:T(8,128)} %get-tuple-element.23) | copy-start | bytes 145924

commit v3 on v2

--- a/solution.py
+++ b/solution.py
@@ -14,7 +14,10 @@
 NY, NZ = 4, 8
 RING = NZ - 1
 LAG = 6
-RING_AT = 4
+RING_AT = 3
+SUM_AT = 8
+SHARED = 16
+TOP, REST = pl.ds(0, 32), pl.ds(32, 16)
 SUBS = ((0, 48), (48, 32))
 EXP_SCALE = 0.125 / math.log(2.0)
 
@@ -46,9 +49,9 @@
 
 def kernel(scale, q_hbm, k_hbm, v_hbm, d_hbm, w_ref, gq_hbm, gk_hbm, gv_hbm, gwo_ref,
            qb, kb, vb, dfull, dcat, doth, wpad, wx, wy, wown, woth, att, lse, osum,
-           dks, dkr, dko, gq_st, gk_st, gv_st, gacc, rss, rsr, gys, gyr, gxs, gxr,
+           dks, dkr, dko, gq_st, gk_st, gv_st, gacc, rss, rsr, gys, gyr, gyf, gxs, gxr,
            q_ld, k_ld, v_ld, d_ld, wx_s, wx_r, wy_s, wy_r, zr_s, zr_r, zl_s, zl_r,
-           oc_s, oc_r, k_s, k_r, v_s, v_r, dx_s, dx_r, at_s, at_r, dk_s, dk_r, dv_s, dv_r,
+           oc_s, oc_r, wp_s, wp_r, k_s, k_r, v_s, v_r, dx_s, dx_r, at_s, at_r, dk_s, dk_r, dv_s, dv_r,
            rr_s, rr_r, rl_s, rl_r, gy_s, gy_r, gx_s, gx_r, gq_o, gk_o, gv_o):
     pairs, toks = qb.shape[0], qb.shape[1]
     cols = wpad.shape[1]
@@ -74,8 +77,10 @@
         return dev(band_=z * NY + lax.rem(y + shift, NY))
 
     cam_peer = dev(cam_=1 - cam)
+    wrap_peer = dev(cam_=1 - cam, obj_=(1 - xh) * 2 + core)
     core_peer = dev(obj_=xh * 2 + 1 - core)
     z_up, z_down = at_z(1), at_z(-1)
+    y_up, y_down = at_y(1), at_y(NY - 1)
 
     def remote(src, dst, send, recv, device):
         return pltpu.make_async_remote_copy(
@@ -119,7 +124,7 @@
     barrier = pltpu.get_barrier_semaphore()
     peers = [dev(cam_=lax.rem(cam + a, 2), obj_=lax.rem(obj + b, 4))
              for a in range(2) for b in range(4) if a + b > 0]
-    peers += [at_y(s) for s in range(1, NY)] + [z_up, z_down]
+    peers += [y_up, y_down, z_up, z_down]
     for peer in peers:
         pl.semaphore_signal(barrier, inc=1, device_id=peer, device_id_type=MESH)
     pl.semaphore_wait(barrier, len(peers))
@@ -151,11 +156,14 @@
     joined = nn(join_x, wx[...].reshape(64, cols)).astype(BF)
     wy[y] = joined
 
-    def y_copy(s):
-        return remote(wy.at[y], wy.at[y], wy_s.at[s], wy_r.at[s], at_y(s))
-
-    for s in range(1, NY):
-        y_copy(s).start()
+    def y_copy(n):
+        block = (y, y, y, y, lax.rem(y + NY - 1, NY), lax.rem(y + 1, NY))[n]
+        rows = (TOP, REST, REST, TOP, TOP, REST)[n]
+        return remote(wy.at[block, rows], wy.at[block, rows], wy_s.at[n], wy_r.at[n],
+                      y_down if n % 2 else y_up)
+
+    for n in range(4):
+        y_copy(n).start()
 
     load_d.wait()
     low, high = dfull[:, 0:cols], dfull[:, cols:2 * cols]
@@ -174,8 +182,11 @@
     d_swap.start()
 
     join_y = picker(blk, 4 * 48, 40, 48, 40)
-    for s in range(1, NY):
-        y_copy(s).wait_recv()
+    for n in range(2):
+        y_copy(n).wait_recv()
+        y_copy(n + 4).start()
+    for n in range(2, 6):
+        y_copy(n).wait_recv()
 
     def block_rows(b, size=None, off=0):
         return pl.ds(pl.multiple_of(b * blk + off, 16), blk if size is None else size)
@@ -184,19 +195,22 @@
 
     def up_copy(h, back):
         b = lax.rem(z - h // 2 - back + NZ, NZ)
-        rows = block_rows(b, half, (h % 2) * half)
+        rows = block_rows(b, half - SHARED, (h % 2) * half + SHARED * xh)
         return remote(wown.at[rows], wown.at[rows], zr_s.at[h], zr_r.at[h], z_up)
 
     def down_copy(h, back):
         b = lax.rem(z + h // 2 + back, NZ)
-        rows = block_rows(b, half, (1 - h % 2) * half)
+        rows = block_rows(b, half - SHARED, (1 - h % 2) * half + SHARED * xh)
         return remote(wown.at[rows], wown.at[rows], zl_s.at[h], zl_r.at[h], z_down)
 
-    def cross(h, up):
+    def cross(h, up, kind=None):
         b = lax.rem(z - h // 2 - 1 + NZ, NZ) if up else lax.rem(z + h // 2 + 1, NZ)
         j = h % 2 if up else 1 - h % 2
+        n = 2 * h + (0 if up else 1)
+        if kind is not None:
+            rows = block_rows(b, SHARED, j * half + (half - SHARED) * kind)
+            return remote(wown.at[rows], wown.at[rows], wp_s.at[n], wp_r.at[n], wrap_peer)
         rows = block_rows(b, half, j * half)
-        n = 2 * h + (0 if up else 1)
         return remote(wown.at[rows], woth.at[rows], oc_s.at[n], oc_r.at[n], core_peer)
 
     own_rows = block_rows(z)
@@ -219,8 +233,8 @@
         def _():
             down_copy(h + 2, 0).start()
 
-        cross(h, True).start()
-        cross(h, False).start()
+        cross(h, True, xh).start()
+        cross(h, False, xh).start()
 
     def split_q(i):
         first, second = halves(qb[i].astype(F32), 1)
@@ -346,7 +360,7 @@
         def _():
             own_term(s + 1)
 
-    @pl.loop(0, pairs + NZ)
+    @pl.loop(0, max(LAG + pairs, SUM_AT + NZ))
     def _(t):
         @pl.when(t < pairs)
         def _():
@@ -358,28 +372,37 @@
         def _():
             cross_own.wait_recv()
 
+        @pl.when((h >= 2) & (h <= RING + 1))
+        def _():
+            cross(h - 2, True).wait_recv()
+            cross(h - 2, False).wait_recv()
+
         @pl.when((h >= 1) & (h <= RING))
         def _():
-            cross(h - 1, True).wait_recv()
-            cross(h - 1, False).wait_recv()
+            for up in (True, False):
+                cross(h - 1, up, 1 - xh).wait_recv()
+                cross(h - 1, up).start()
 
         @pl.when((h >= 0) & (h < RING))
         def _():
             ring(h)
 
-        s = t - pairs
+        @pl.when((t >= 1) & (t < pairs))
+        def _():
+            swap_att(t - 1).wait_recv()
+
+        @pl.when(t == pairs - 1)
+        def _():
+            swap_att(t).wait_recv()
+
+        s = t - SUM_AT
 
         @pl.when(s == 0)
         def _():
             d_swap.wait_recv()
-
-            @pl.loop(0, pairs)
-            def _(i):
-                swap_att(i).wait_recv()
-
             own_term(0)
 
-        @pl.when(s >= 0)
+        @pl.when((s >= 0) & (s < NZ))
         def _():
             sum_step(s)
 
@@ -387,21 +410,38 @@
         def _():
             backward(t - LAG)
 
-    def sum_y(s):
-        return remote(gys.at[lax.rem(y + s, NY)], gyr.at[s], gy_s.at[s], gy_r.at[s], at_y(s))
+    y_next, y_last = lax.rem(y + 1, NY), lax.rem(y + NY - 1, NY)
+    y_far = lax.rem(y + 2, NY)
+
+    def sum_y(n):
+        rows = (TOP, REST, REST, TOP, TOP, REST)[n]
+        src = (gys.at[y_far], gys.at[y_far], gys.at[y_next], gys.at[y_last], gyf, gyf)[n]
+        dst = (0, 1, 2, 3, 2, 3)[n]
+        return remote(src.at[rows], gyr.at[dst, rows], gy_s.at[n], gy_r.at[n],
+                      y_down if n % 2 else y_up)
 
     gys[...] = nn(picker(4 * 48, blk, 48, 40, 40), gacc[...].astype(BF)).astype(BF).reshape(4, 48, cols)
-    for s in range(1, NY):
-        sum_y(s).start()
-
-    @pl.loop(0, pairs - 3)
+    for n in range(4):
+        sum_y(n).start()
+
+    @pl.loop(0, pairs - 6)
     def _(i):
         finish(i)
 
-    summed = gys[y].astype(F32)
-    for s in range(1, NY):
-        sum_y(s).wait_recv()
-        summed = summed + gyr[s].astype(F32)
+    sum_y(0).wait_recv()
+    gyf[0:32] = (gys[y_next, 0:32].astype(F32) + gyr[0, 0:32].astype(F32)).astype(BF)
+    sum_y(4).start()
+    sum_y(1).wait_recv()
+    gyf[32:48] = (gys[y_last, 32:48].astype(F32) + gyr[1, 32:48].astype(F32)).astype(BF)
+    sum_y(5).start()
+
+    @pl.loop(pairs - 6, pairs - 3)
+    def _(i):
+        finish(i)
+
+    for n in range(2, 6):
+        sum_y(n).wait_recv()
+    summed = gys[y].astype(F32) + gyr[2].astype(F32) + gyr[3].astype(F32)
     gxs[...] = nn(picker(64, 48, 16, 10, 10), summed.astype(BF)).astype(BF).reshape(4, 16, cols)
 
     def sum_x(o):
@@ -436,9 +476,9 @@
         def _():
             sum_x(t).wait_send()
 
-    for s in range(1, NY):
-        y_copy(s).wait_send()
-        sum_y(s).wait_send()
+    for n in range(6):
+        y_copy(n).wait_send()
+        sum_y(n).wait_send()
     d_swap.wait_send()
     cross_own.wait_send()
 
@@ -446,8 +486,9 @@
     def _(h):
         up_copy(h, 0).wait_send()
         down_copy(h, 0).wait_send()
-        cross(h, True).wait_send()
-        cross(h, False).wait_send()
+        for up in (True, False):
+            cross(h, up).wait_send()
+            cross(h, up, xh).wait_send()
         for sub in range(len(SUBS)):
             sum_up(h, sub).wait_send()
             sum_down(h, sub).wait_send()
@@ -504,14 +545,15 @@
         pltpu.VMEM((RING, 2, blk // 2, cols), BF),
         pltpu.VMEM((4, 48, cols), BF),
         pltpu.VMEM((4, 48, cols), BF),
+        pltpu.VMEM((48, cols), BF),
         pltpu.VMEM((4, 16, cols), BF),
         pltpu.VMEM((4, 16, cols), BF),
         dma(pairs), dma(pairs), dma(pairs), pltpu.SemaphoreType.DMA,
-        dma(4), dma(4), dma(4), dma(4), dma(RING), dma(RING), dma(RING), dma(RING),
-        dma(2 * RING + 1), dma(2 * RING + 1), dma(pairs), dma(pairs), dma(pairs), dma(pairs),
+        dma(4), dma(4), dma(6), dma(6), dma(RING), dma(RING), dma(RING), dma(RING),
+        dma(2 * RING + 1), dma(2 * RING + 1), dma(2 * RING), dma(2 * RING), dma(pairs), dma(pairs), dma(pairs), dma(pairs),
         pltpu.SemaphoreType.DMA, pltpu.SemaphoreType.DMA, dma(pairs), dma(pairs),
         dma(pairs), dma(pairs), dma(pairs), dma(pairs),
-        dma(RING, 2), dma(RING, 2), dma(RING, 2), dma(RING, 2), dma(4), dma(4), dma(4), dma(4),
+        dma(RING, 2), dma(RING, 2), dma(RING, 2), dma(RING, 2), dma(6), dma(6), dma(4), dma(4),
         dma(pairs), dma(pairs), dma(pairs),
     ]
     gq, gk, gv, gwo = pl.pallas_call(

time: 120 us -> 118 us (0.983)
  Pallas kernels: 114 us -> 112 us
    pallas_call x1, Pallas kernels: 114 us -> 112 us  [body(): pl.pallas_call(functools.partial(kernel, scale), out_shape=(grad, grad, g...]
where the time goes in v3:
time: 118 us
  Pallas kernels  112 us (95%)
  local copies, waits for them, and re-layouts  4.88 us (4%)
    pallas_call x1, Pallas kernels, body(): pl.pallas_call(functools.partial(kernel, scale), out_shape=(grad, grad, g...  112 us
    unnamed x10, local copies, waits for them, and re-layouts  4.88 us

profile of v3, /device:TPU:1, one launch (start us, length us, event | category | flops | bytes accessed | tf_op | source)
XLA Modules:
  0.0 117.5 jit_solution(15268052195039954373)
XLA Ops:
  0.6 112.0 %row_attention_backward.1 = (bf16[384,1280]{1,0:T(8,128)(2,1)}, bf16[384,1280]{1,0:T(8,128)(2,1)}, bf16[384,1280]{1,0:T(8,128)(2,1)}, f32[10,1216]{1,0:T(8,128)}) custom-call(bf16[384,1280]{1,0:T(8,128)(2,1)} %bitcast.14, bf16[384,1280]{1,0:T(8,128)(2,1)} %bitcast.15, bf16[384,1280]{1,0:T(8,128)(2,1)} %bitcast.16, bf16[384,2432]{1,0:T(8,128)(2,1)} %bitcast.13, ...), custom_call_target="tpu_custom_call" | custom-call | tf_op jit(solution)/shard_map/row_attention_backward/pallas_call | solution.py:559
  112.6 0.0 copy-start.1
  112.6 0.0 copy-start
  112.7 2.3 %copy.16 = bf16[1,3,1,128,1280]{4,3,2,1,0:T(8,128)(2,1)} copy(bf16[1,3,1,128,1280]{4,3,2,1,0:T(8,128)(2,1)} %bitcast.19) | data formatting | bytes 1966080
  115.0 0.0 copy-done.1
  115.0 0.0 copy-start.2
  115.0 0.9 copy.17
  116.0 0.0 copy-done
  116.0 0.9 copy.18
  116.9 0.0 copy-done.2
  116.9 0.6 copy.19
Async XLA Ops:
  112.6 2.4 %copy-start.1 = (bf16[384,1280]{1,0:T(8,128)(2,1)S(1)}, bf16[384,1280]{1,0:T(8,128)(2,1)}, u32[]{:S(2)}) copy-start(bf16[384,1280]{1,0:T(8,128)(2,1)} %get-tuple-element.9) | copy-start | bytes 2949124
  112.6 3.3 %copy-start = (bf16[384,1280]{1,0:T(8,128)(2,1)S(1)}, bf16[384,1280]{1,0:T(8,128)(2,1)}, u32[]{:S(2)}) copy-start(bf16[384,1280]{1,0:T(8,128)(2,1)} %get-tuple-element.10) | copy-start | bytes 2949124
  115.0 1.9 %copy-start.2 = (f32[10,1216]{1,0:T(8,128)S(1)}, f32[10,1216]{1,0:T(8,128)}, u32[]{:S(2)}) copy-start(f32[10,1216]{1,0:T(8,128)} %get-tuple-element.23) | copy-start | bytes 145924

commit v4 on v3

--- a/solution.py
+++ b/solution.py
@@ -341,24 +341,20 @@
                                 att[block_rows(owner_down, half, half), :]], axis=0)
         gacc[...] = nn(rows, dcat[...])
 
-    def sum_step(s):
-        for sub, (off, size) in enumerate(SUBS):
-            for way, copy in enumerate((sum_up, sum_down)):
-                at = slice(way * half + off, way * half + off + size)
-
-                @pl.when(s > 0)
-                def _():
-                    copy(s - 1, sub).wait_recv()
-                    gacc[at, :] = gacc[at, :] + rsr[s - 1, way, off:off + size].astype(F32)
-
-                @pl.when(s < RING)
-                def _():
-                    rss[s, way, off:off + size] = gacc[at, :].astype(BF)
-                    copy(s, sub).start()
-
-        @pl.when(s < RING)
-        def _():
-            own_term(s + 1)
+    def sum_step(s, sub):
+        off, size = SUBS[sub]
+        for way, copy in enumerate((sum_up, sum_down)):
+            at = slice(way * half + off, way * half + off + size)
+
+            @pl.when(s > 0)
+            def _():
+                copy(s - 1, sub).wait_recv()
+                gacc[at, :] = gacc[at, :] + rsr[s - 1, way, off:off + size].astype(F32)
+
+            @pl.when(s < RING)
+            def _():
+                rss[s, way, off:off + size] = gacc[at, :].astype(BF)
+                copy(s, sub).start()
 
     @pl.loop(0, max(LAG + pairs, SUM_AT + NZ))
     def _(t):
@@ -404,11 +400,19 @@
 
         @pl.when((s >= 0) & (s < NZ))
         def _():
-            sum_step(s)
+            sum_step(s, 0)
 
         @pl.when((t >= LAG) & (t < LAG + pairs))
         def _():
             backward(t - LAG)
+
+        @pl.when((s >= 0) & (s < NZ))
+        def _():
+            sum_step(s, 1)
+
+        @pl.when((s >= 0) & (s < RING))
+        def _():
+            own_term(s + 1)
 
     y_next, y_last = lax.rem(y + 1, NY), lax.rem(y + NY - 1, NY)
     y_far = lax.rem(y + 2, NY)

time: 118 us -> 116 us (0.983)
  Pallas kernels: 112 us -> 110 us
    pallas_call x1, Pallas kernels: 112 us -> 110 us  [body(): pl.pallas_call(functools.partial(kernel, scale), out_shape=(grad, grad, g...]
where the time goes in v4:
time: 116 us; the launch traced here: 115 us
  Pallas kernels  110 us (95%)
  local copies, waits for them, and re-layouts  4.88 us (4%)
    pallas_call x1, Pallas kernels, body(): pl.pallas_call(functools.partial(kernel, scale), out_shape=(grad, grad, g...  110 us
    unnamed x10, local copies, waits for them, and re-layouts  4.88 us

profile of v4, /device:TPU:1, one launch (start us, length us, event | category | flops | bytes accessed | tf_op | source)
XLA Modules:
  0.0 115.5 jit_solution(12965401709499727875)
XLA Ops:
  0.6 109.9 %row_attention_backward.1 = (bf16[384,1280]{1,0:T(8,128)(2,1)}, bf16[384,1280]{1,0:T(8,128)(2,1)}, bf16[384,1280]{1,0:T(8,128)(2,1)}, f32[10,1216]{1,0:T(8,128)}) custom-call(bf16[384,1280]{1,0:T(8,128)(2,1)} %bitcast.14, bf16[384,1280]{1,0:T(8,128)(2,1)} %bitcast.15, bf16[384,1280]{1,0:T(8,128)(2,1)} %bitcast.16, bf16[384,2432]{1,0:T(8,128)(2,1)} %bitcast.13, ...), custom_call_target="tpu_custom_call" | custom-call | tf_op jit(solution)/shard_map/row_attention_backward/pallas_call | solution.py:563
  110.6 0.0 copy-start.1
  110.6 0.0 copy-start
  110.6 2.3 %copy.16 = bf16[1,3,1,128,1280]{4,3,2,1,0:T(8,128)(2,1)} copy(bf16[1,3,1,128,1280]{4,3,2,1,0:T(8,128)(2,1)} %bitcast.19) | data formatting | bytes 1966080
  113.0 0.0 copy-done.1
  113.0 0.0 copy-start.2
  113.0 0.9 copy.17
  113.9 0.0 copy-done
  113.9 0.9 copy.18
  114.9 0.0 copy-done.2
  114.9 0.6 copy.19
Async XLA Ops:
  110.6 2.4 %copy-start.1 = (bf16[384,1280]{1,0:T(8,128)(2,1)S(1)}, bf16[384,1280]{1,0:T(8,128)(2,1)}, u32[]{:S(2)}) copy-start(bf16[384,1280]{1,0:T(8,128)(2,1)} %get-tuple-element.9) | copy-start | bytes 2949124
  110.6 3.3 %copy-start = (bf16[384,1280]{1,0:T(8,128)(2,1)S(1)}, bf16[384,1280]{1,0:T(8,128)(2,1)}, u32[]{:S(2)}) copy-start(bf16[384,1280]{1,0:T(8,128)(2,1)} %get-tuple-element.10) | copy-start | bytes 2949124
  113.0 1.9 %copy-start.2 = (f32[10,1216]{1,0:T(8,128)S(1)}, f32[10,1216]{1,0:T(8,128)}, u32[]{:S(2)}) copy-start(f32[10,1216]{1,0:T(8,128)} %get-tuple-element.23) | copy-start | bytes 145924

commit v5 on v4

--- a/solution.py
+++ b/solution.py
@@ -227,13 +227,15 @@
         def _():
             up_copy(h + 2, 0).start()
 
+        cross(h, True, xh).start()
+
+    def ring_down(h):
         down_copy(h, 1).wait_recv()
 
         @pl.when(h + 2 < RING)
         def _():
             down_copy(h + 2, 0).start()
 
-        cross(h, True, xh).start()
         cross(h, False, xh).start()
 
     def split_q(i):
@@ -358,11 +360,26 @@
 
     @pl.loop(0, max(LAG + pairs, SUM_AT + NZ))
     def _(t):
+        s = t - SUM_AT
+
+        @pl.when(s == 0)
+        def _():
+            d_swap.wait_recv()
+            own_term(0)
+
+        @pl.when((s >= 0) & (s < NZ))
+        def _():
+            sum_step(s, 0)
+
+        h = t - RING_AT
+
+        @pl.when((h >= 0) & (h < RING))
+        def _():
+            ring(h)
+
         @pl.when(t < pairs)
         def _():
             forward(t)
-
-        h = t - RING_AT
 
         @pl.when(h == 0)
         def _():
@@ -381,7 +398,7 @@
 
         @pl.when((h >= 0) & (h < RING))
         def _():
-            ring(h)
+            ring_down(h)
 
         @pl.when((t >= 1) & (t < pairs))
         def _():
@@ -390,17 +407,6 @@
         @pl.when(t == pairs - 1)
         def _():
             swap_att(t).wait_recv()
-
-        s = t - SUM_AT
-
-        @pl.when(s == 0)
-        def _():
-            d_swap.wait_recv()
-            own_term(0)
-
-        @pl.when((s >= 0) & (s < NZ))
-        def _():
-            sum_step(s, 0)
 
         @pl.when((t >= LAG) & (t < LAG + pairs))
         def _():

time: 116 us -> 115 us (level)
  no operation moved by 1% of the time
where the time goes in v5:
time: 115 us
  Pallas kernels  109 us (95%)
  local copies, waits for them, and re-layouts  4.88 us (4%)
    pallas_call x1, Pallas kernels, body(): pl.pallas_call(functools.partial(kernel, scale), out_shape=(grad, grad, g...  109 us
    unnamed x10, local copies, waits for them, and re-layouts  4.88 us

profile of v5, /device:TPU:1, one launch (start us, length us, event | category | flops | bytes accessed | tf_op | source)
XLA Modules:
  0.0 114.7 jit_solution(15648702041623252216)
XLA Ops:
  0.6 109.2 %row_attention_backward.1 = (bf16[384,1280]{1,0:T(8,128)(2,1)}, bf16[384,1280]{1,0:T(8,128)(2,1)}, bf16[384,1280]{1,0:T(8,128)(2,1)}, f32[10,1216]{1,0:T(8,128)}) custom-call(bf16[384,1280]{1,0:T(8,128)(2,1)} %bitcast.14, bf16[384,1280]{1,0:T(8,128)(2,1)} %bitcast.15, bf16[384,1280]{1,0:T(8,128)(2,1)} %bitcast.16, bf16[384,2432]{1,0:T(8,128)(2,1)} %bitcast.13, ...), custom_call_target="tpu_custom_call" | custom-call | tf_op jit(solution)/shard_map/row_attention_backward/pallas_call | solution.py:569
  109.8 0.0 copy-start.1
  109.8 0.0 copy-start
  109.8 2.3 %copy.16 = bf16[1,3,1,128,1280]{4,3,2,1,0:T(8,128)(2,1)} copy(bf16[1,3,1,128,1280]{4,3,2,1,0:T(8,128)(2,1)} %bitcast.19) | data formatting | bytes 1966080
  112.2 0.0 copy-done.1
  112.2 0.0 copy-start.2
  112.2 0.9 copy.17
  113.1 0.0 copy-done
  113.1 0.9 copy.18
  114.1 0.0 copy-done.2
  114.1 0.6 copy.19
Async XLA Ops:
  109.8 2.4 %copy-start.1 = (bf16[384,1280]{1,0:T(8,128)(2,1)S(1)}, bf16[384,1280]{1,0:T(8,128)(2,1)}, u32[]{:S(2)}) copy-start(bf16[384,1280]{1,0:T(8,128)(2,1)} %get-tuple-element.9) | copy-start | bytes 2949124
  109.8 3.3 %copy-start = (bf16[384,1280]{1,0:T(8,128)(2,1)S(1)}, bf16[384,1280]{1,0:T(8,128)(2,1)}, u32[]{:S(2)}) copy-start(bf16[384,1280]{1,0:T(8,128)(2,1)} %get-tuple-element.10) | copy-start | bytes 2949124
  112.2 1.9 %copy-start.2 = (f32[10,1216]{1,0:T(8,128)S(1)}, f32[10,1216]{1,0:T(8,128)}, u32[]{:S(2)}) copy-start(f32[10,1216]{1,0:T(8,128)} %get-tuple-element.23) | copy-start | bytes 145924
